TPU v7x, 128 devices: a whole 4x4x4 slice. The times are simulated.
128 devices in a mesh: req: 8 (over z, core), tok: 16 (over y, x).
Axes of the slice: x: 4, y: 4, z: 4, core: 2. Of those that a mesh axis runs over, the one named last changes fastest.
Arguments:
- draft_ids: int32 [32, 16], replicated, may hold values from 0 to 65535
- lengths: int32 [32], replicated, may hold values from 1 to 16384, as said below
- current_slot: int32 [32], replicated, may hold values from 0 to 31, as said below
- new_slot: int32 [32], replicated, may hold values from 0 to 31, as said below
- accepted: int32 [32], replicated, may hold values from 1 to 16, as said below
- embed_table: bfloat16 [65536, 3072], P(('req', 'tok')), may hold values from -6.5 to 6.5
- mixer_gain: float32 [3072], replicated, may hold values from 0.5 to 1.5
- query_weight: bfloat16 [3072, 768], replicated, may hold values from -0.3049512 to 0.3049512
- keyvalue_weight: bfloat16 [3072, 256], replicated, may hold values from -0.109375 to 0.109375
- key_cache: bfloat16 [32, 16384, 128], P('req', 'tok'), may hold values from -6 to 6
- value_cache: bfloat16 [32, 16384, 128], P('req', 'tok'), may hold values from -6 to 6
- attention_out: bfloat16 [768, 3072], P(None, 'tok'), may hold values from -0.21875 to 0.21875
- mamba_input: bfloat16 [3072, 2048], P(None, 'tok'), may hold values from -0.109375 to 0.109375
- mamba_gate: bfloat16 [3072, 2048], P(None, 'tok'), may hold values from -0.109375 to 0.109375
- state_proj: bfloat16 [3072, 512], replicated, may hold values from -0.02734375 to 0.02734375
- mamba_step: bfloat16 [3072, 16], P(None, 'tok'), may hold values from -0.109375 to 0.109375
- step_bias: float32 [16], P('tok'), may hold values from -4 to 0
- decay_log: float32 [16], P('tok'), may hold values from -2 to 1.5
- skip_gain: float32 [16], P('tok'), may hold values from 0.5 to 1.5
- states: float32 [32, 16, 128, 256], P('req', 'tok'), may hold values from -1.5 to 1.5
- mamba_out: bfloat16 [2048, 3072], P('tok'), may hold values from -0.125 to 0.125
- mlp_gain: float32 [3072], replicated, may hold values from 0.5 to 1.5
- gate_weight: bfloat16 [3072, 12288], P(None, ('req', 'tok')), may hold values from -0.109375 to 0.109375
- up_weight: bfloat16 [3072, 12288], P(None, ('req', 'tok')), may hold values from -0.109375 to 0.109375
- down_weight: bfloat16 [3072, 12288], P(None, ('req', 'tok')), may hold values from -0.0546875 to 0.0546875
Outputs:
- hidden_out: bfloat16 [512, 3072], P(('req', 'tok'))
- new_states: float32 [32, 16, 128, 256], P('req', 'tok')
Inputs may be any that keep to these rules, and one draw needn't show every extreme that they name: `lengths`: some request has exactly 16384 cached positions and some exactly one. `current_slot`: a permutation: each slot holds one request. `new_slot`: a permutation: each slot receives one request. `accepted`: some request accepts all 16 drafts and some exactly one.
All inputs are finite; a program needn't handle non-finite values.
Results may differ from a plain program's by a relative error of at most 0.02.
Values may be sent and summed in bfloat16 or wider, within the bound.
No kernel may reach another device: no remote copies, remote signals or barrier semaphores. Data moves between devices by JAX's collectives and lax.ppermute only.
A program may use at most 128 MiB of HBM per device.

v0:
```python
import jax
import jax.numpy as jnp
from jax import lax
from jax.sharding import PartitionSpec as P


def rms_rows(table_rows, norm_gain):
    values = table_rows.astype(jnp.float32)
    factor = lax.rsqrt(jnp.mean(values * values, axis=-1, keepdims=True) + 1e-05)
    return (values * factor * norm_gain).astype(jnp.bfloat16)


def inverse_of(mapping):
    places = jnp.arange(mapping.shape[0], dtype=jnp.int32)
    matches = mapping[None, :] == places[:, None]
    return jnp.sum(jnp.where(matches, places[None, :], 0), axis=1)


def recurrence(start_states, decay_rate, inputs, state_in, state_read, accept_count):

    def advance(state_pair, step_items):
        current, chosen = state_pair
        step_decay, step_input, step_in, step_read, step_index = step_items
        current = (
            step_decay[:, :, None, None] * current
            + step_input[..., None] * step_in[:, None, None, :]
        )
        readout = jnp.sum(current * step_read[:, None, None, :], axis=-1)
        chosen = jnp.where((accept_count == step_index + 1)[:, None, None, None], current, chosen)
        return ((current, chosen), readout)

    sequence = (
        jnp.swapaxes(decay_rate, 0, 1),
        jnp.swapaxes(inputs, 0, 1),
        jnp.swapaxes(state_in, 0, 1),
        jnp.swapaxes(state_read, 0, 1),
        jnp.arange(decay_rate.shape[1], dtype=jnp.int32),
    )
    (current, chosen), readouts = lax.scan(advance, (start_states, start_states), sequence)
    return (jnp.swapaxes(readouts, 0, 1), chosen)


def feed_units(block_rows, gate_cols, up_cols, down_cols):
    gate_part = jnp.dot(block_rows, gate_cols, preferred_element_type=jnp.float32)
    up_part = jnp.dot(block_rows, up_cols, preferred_element_type=jnp.float32)
    hidden = (jax.nn.silu(gate_part) * up_part).astype(jnp.bfloat16)
    return lax.dot_general(
        hidden, down_cols, (((1,), (1,)), ((), ())), preferred_element_type=jnp.float32
    )


def local(
    draft_ids,
    lengths,
    current_slot,
    new_slot,
    accepted,
    embed_table,
    mixer_gain,
    query_weight,
    keyvalue_weight,
    key_cache,
    value_cache,
    attention_out,
    mamba_input,
    mamba_gate,
    state_proj,
    mamba_step,
    step_bias,
    decay_log,
    skip_gain,
    states,
    mamba_out,
    mlp_gain,
    gate_weight,
    up_weight,
    down_weight,
):
    members = lax.axis_size("tok")
    group_index = lax.axis_index("req")
    member = lax.axis_index("tok")
    slots_dev, cache_dev, head_size = key_cache.shape
    draft_len = draft_ids.shape[1]
    group_tokens = slots_dev * draft_len
    vocab_dev = embed_table.shape[0]
    query_heads = query_weight.shape[1] // head_size
    heads_dev = step_bias.shape[0]
    mamba_head = mamba_input.shape[1] // heads_dev
    state_size = state_proj.shape[1] // 2
    slot_owner = inverse_of(current_slot)
    token_ids = jnp.take(draft_ids, slot_owner, axis=0).reshape(-1)
    vocab_start = (group_index * members + member) * vocab_dev
    wanted = token_ids - vocab_start
    inside = (wanted >= 0) & (wanted < vocab_dev)
    picked = jnp.take(embed_table, jnp.clip(wanted, 0, vocab_dev - 1), axis=0)
    embedded = lax.psum_scatter(
        jnp.where(inside[:, None], picked.astype(jnp.float32), 0.0),
        ("req", "tok"),
        scatter_dimension=0,
        tiled=True,
    ).astype(jnp.bfloat16)
    normed = rms_rows(embedded, mixer_gain)
    gathered = lax.all_gather(normed, "tok", axis=0, tiled=True)
    queries = jnp.dot(gathered, query_weight, preferred_element_type=jnp.float32).astype(
        jnp.bfloat16
    )
    queries = queries.reshape(slots_dev, draft_len, query_heads, head_size)
    keyvalue = jnp.dot(gathered, keyvalue_weight, preferred_element_type=jnp.float32).astype(
        jnp.bfloat16
    )
    keyvalue = keyvalue.reshape(slots_dev, draft_len, 2, head_size)
    local_owner = lax.dynamic_slice_in_dim(slot_owner, group_index * slots_dev, slots_dev)
    slot_length = jnp.take(lengths, local_owner)
    slot_accept = jnp.take(accepted, local_owner)
    score_scale = head_size ** (-0.5)
    positions = member * cache_dev + jnp.arange(cache_dev, dtype=jnp.int32)
    visible = (positions[None, :] < slot_length[:, None])[:, None, None, :]
    cache_scores = (
        jnp.einsum("sthd,spd->sthp", queries, key_cache, preferred_element_type=jnp.float32)
        * score_scale
    )
    local_max = jnp.max(jnp.where(visible, cache_scores, -1e30), axis=-1)
    cache_probs = jnp.where(visible, jnp.exp(cache_scores - local_max[..., None]), 0.0)
    local_total = jnp.sum(cache_probs, axis=-1)
    local_out = jnp.einsum(
        "sthp,spd->sthd",
        cache_probs.astype(jnp.bfloat16),
        value_cache,
        preferred_element_type=jnp.float32,
    )
    cache_max = lax.pmax(local_max, "tok")
    factor = jnp.exp(local_max - cache_max)
    cache_total, cache_out = (
        lax.psum((local_total * factor).astype(jnp.bfloat16), "tok").astype(jnp.float32),
        lax.psum((local_out * factor[..., None]).astype(jnp.bfloat16), "tok").astype(jnp.float32),
    )
    causal = (jnp.arange(draft_len)[None, :] <= jnp.arange(draft_len)[:, None])[None, :, None, :]
    draft_scores = (
        jnp.einsum("sthd,sud->sthu", queries, keyvalue[:, :, 0], preferred_element_type=jnp.float32)
        * score_scale
    )
    draft_max = jnp.max(jnp.where(causal, draft_scores, -1e30), axis=-1)
    joint_max = jnp.maximum(cache_max, draft_max)
    cache_factor = jnp.exp(cache_max - joint_max)
    draft_probs = jnp.where(causal, jnp.exp(draft_scores - joint_max[..., None]), 0.0)
    prob_total = cache_total * cache_factor + jnp.sum(draft_probs, axis=-1)
    summed = cache_out * cache_factor[..., None] + jnp.einsum(
        "sthu,sud->sthd",
        draft_probs.astype(jnp.bfloat16),
        keyvalue[:, :, 1],
        preferred_element_type=jnp.float32,
    )
    attended = (
        (summed / prob_total[..., None])
        .astype(jnp.bfloat16)
        .reshape(group_tokens, query_heads * head_size)
    )
    attn_proj = jnp.dot(attended, attention_out, preferred_element_type=jnp.float32)
    attn_rows = lax.all_to_all(
        attn_proj.astype(jnp.bfloat16), "tok", split_axis=0, concat_axis=1, tiled=True
    ).astype(attn_proj.dtype)
    mamba_x = jnp.dot(gathered, mamba_input, preferred_element_type=jnp.float32)
    mamba_x = mamba_x.reshape(slots_dev, draft_len, heads_dev, mamba_head)
    mamba_z = jnp.dot(gathered, mamba_gate, preferred_element_type=jnp.float32)
    mamba_z = mamba_z.reshape(slots_dev, draft_len, heads_dev, mamba_head)
    both_proj = jnp.dot(gathered, state_proj, preferred_element_type=jnp.float32)
    both_proj = both_proj.reshape(slots_dev, draft_len, 2, state_size)
    step_size = jax.nn.softplus(
        jnp.dot(gathered, mamba_step, preferred_element_type=jnp.float32) + step_bias
    ).reshape(slots_dev, draft_len, heads_dev)
    decay_rate = jnp.exp(-jnp.exp(decay_log) * step_size)
    readout, chosen = recurrence(
        states,
        decay_rate,
        step_size[..., None] * mamba_x,
        both_proj[:, :, 0],
        both_proj[:, :, 1],
        slot_accept,
    )
    readout = readout + skip_gain[None, None, :, None] * mamba_x
    gated = (
        (readout * jax.nn.silu(mamba_z))
        .astype(jnp.bfloat16)
        .reshape(group_tokens, heads_dev * mamba_head)
    )
    mamba_rows = lax.psum_scatter(
        jnp.dot(gated, mamba_out, preferred_element_type=jnp.float32).astype(jnp.bfloat16),
        "tok",
        scatter_dimension=0,
        tiled=True,
    ).astype(jnp.float32)
    mixed_rows = (embedded.astype(jnp.float32) + attn_rows + mamba_rows).astype(jnp.bfloat16)
    second = rms_rows(mixed_rows, mlp_gain)
    everything = lax.all_gather(second, ("req", "tok"), axis=0, tiled=True)
    mlp_rows = lax.psum_scatter(
        feed_units(everything, gate_weight, up_weight, down_weight),
        ("req", "tok"),
        scatter_dimension=0,
        tiled=True,
    )
    hidden_out = (mixed_rows.astype(jnp.float32) + mlp_rows).astype(jnp.bfloat16)
    every_state = lax.all_gather(chosen.astype(jnp.bfloat16), "req", axis=0, tiled=True).astype(
        chosen.dtype
    )
    incoming = inverse_of(new_slot)
    local_targets = lax.dynamic_slice_in_dim(incoming, group_index * slots_dev, slots_dev)
    sources = jnp.take(current_slot, local_targets)
    new_states = jnp.take(every_state, sources, axis=0)
    return (hidden_out, new_states)


def solution(mesh):
    return jax.shard_map(
        local,
        mesh=mesh,
        in_specs=(
            P(),
            P(),
            P(),
            P(),
            P(),
            P(("req", "tok"), None),
            P(),
            P(),
            P(),
            P("req", "tok", None),
            P("req", "tok", None),
            P(None, "tok"),
            P(None, "tok"),
            P(None, "tok"),
            P(),
            P(None, "tok"),
            P("tok"),
            P("tok"),
            P("tok"),
            P("req", "tok", None, None),
            P("tok", None),
            P(),
            P(None, ("req", "tok")),
            P(None, ("req", "tok")),
            P(None, ("req", "tok")),
        ),
        out_specs=(P(("req", "tok"), None), P("req", "tok", None, None)),
        check_vma=False,
    )
```

profile of v0, /device:TPU:1, one launch (start us, length us, event | category | flops | bytes accessed | tf_op | source)
XLA Modules:
  0.0 808.4 jit_solution(15467223869452533136)
XLA Ops:
  7.2 2.0 copy.142
  12.4 3.9 gather_fusion.1
  16.4 6.2 convert_select_fusion
  22.5 109.7 %all-reduce.11 = bf16[512,3072]{1,0:T(8,128)(2,1)} all-reduce(f32[512,3072]{1,0:T(8,128)} %convert_select_fusion), channel_id=2, replica_groups=mesh['req'=8,'tok'=16] {'req','tok'}, use_global_device_ids=true, to_apply=%region_1.2.clone | all-reduce | flops 1572864 | bytes 9437184
  133.7 19.8 %all-gather = bf16[16,4,3072]{2,1,0:T(4,128)(2,1)} all-gather(bf16[1,4,3072]{2,1,0:T(4,128)(2,1)S(1)} %fusion.44), channel_id=1, replica_groups=mesh['req'=8,'tok'=16] {'tok'}, dimensions={0}, use_global_device_ids=true | all-gather | bytes 417792 | tf_op jit(solution)/shard_map/all_gather | solution.py:103
  154.7 3.9 convolution_convert_fusion.1
  158.6 1.7 reshape.337
  166.3 2.9 select_reduce_fusion
  169.2 57.9 %pmax.7 = f32[4,16,6]{1,2,0:T(8,128)} all-reduce(f32[4,16,6]{1,2,0:T(8,128)S(1)} %get-tuple-element.145), channel_id=1, replica_groups=mesh['req'=8,'tok'=16] {'tok'}, use_global_device_ids=true, to_apply=%region_4.6 | all-reduce | flops 384 | bytes 3072 | tf_op jit(solution)/shard_map/pmax | solution.py:131
  227.1 2.4 fusion.1
  229.5 2.4 convolution_convert_fusion.2
  234.8 3.2 fusion.54
  239.6 1.8 fusion.51
  241.3 2.0 fusion.53
  250.2 1.8 convert.11
  255.5 165.3 %while.14 = (s32[]{:T(128)}, f32[4,1,128,256]{3,2,1,0:T(8,128)}, bf16[4,1,128,256]{3,2,1,0:T(8,128)(2,1)}, f32[16,4,1,128]{3,0,1,2:T(8,128)}, f32[16,4,1]{1,2,0:...) while((s32[]{:T(128)}, f32[4,1,128,256]{3,2,1,0:T(8,128)}, ...), condition=%wide.region_12.14_spmd, body=%wide.region_10.13_spmd.sunk | while | flops 785927 | bytes 2134257 | solution.py:39
  257.6 2.6 multiply_reduce_fusion.2
  262.6 1.9 broadcast_select_fusion.4
  268.0 2.6 multiply_reduce_fusion.2
  273.0 1.9 broadcast_select_fusion.4
  278.3 2.6 multiply_reduce_fusion.2
  283.3 1.9 broadcast_select_fusion.4
  288.7 2.6 multiply_reduce_fusion.2
  293.7 1.9 broadcast_select_fusion.4
  299.1 2.6 multiply_reduce_fusion.2
  304.1 1.9 broadcast_select_fusion.4
  309.4 2.6 multiply_reduce_fusion.2
  314.4 1.9 broadcast_select_fusion.4
  319.6 2.6 multiply_reduce_fusion.2
  324.7 1.9 broadcast_select_fusion.4
  330.0 2.6 multiply_reduce_fusion.2
  335.0 1.9 broadcast_select_fusion.4
  340.3 2.6 multiply_reduce_fusion.2
  345.4 1.9 broadcast_select_fusion.4
  350.6 2.6 multiply_reduce_fusion.2
  355.6 1.9 broadcast_select_fusion.4
  361.0 2.6 multiply_reduce_fusion.2
  366.0 1.9 broadcast_select_fusion.4
  371.3 2.6 multiply_reduce_fusion.2
  376.3 1.9 broadcast_select_fusion.4
  381.6 2.6 multiply_reduce_fusion.2
  386.6 1.9 broadcast_select_fusion.4
  391.9 2.6 multiply_reduce_fusion.2
  396.9 1.9 broadcast_select_fusion.4
  402.3 2.6 multiply_reduce_fusion.2
  407.3 1.9 broadcast_select_fusion.4
  412.6 2.6 multiply_reduce_fusion.2
  417.6 1.9 broadcast_select_fusion.4
  422.9 2.0 select_reduce_fusion.1
  425.7 2.2 convolution_convert_fusion
  428.6 2.8 fusion.5
  431.4 29.1 %psum.15 = bf16[4,16,6]{1,2,0:T(8,128)(2,1)S(1)} all-reduce(bf16[4,16,6]{1,2,0:T(8,128)(2,1)S(1)} %get-tuple-element.132), channel_id=1, replica_groups=mesh['req'=8,'tok'=16] {'tok'}, use_global_device_ids=true, to_apply=%region_8.10 | all-reduce | flops 384 | bytes 1536 | tf_op jit(solution)/shard_map/psum | solution.py:134
  462.2 68.0 %all-reduce.10.cloned.1.call-done = (bf16[4,16,6,128]{3,1,2,0:T(8,128)(2,1)}, bf16[64,3072]{1,0:T(8,128)(2,1)}) async-done(((bf16[4,16,6,128]{3,1,2,0:T(8,128)(2,1)}, bf16[64,3072]{1,0:T(8,128)(2,1)}), (bf16[4,16,6,128]{3,1,2,0:T(8,128)(2,1)}, bf16[64,3072]{1,0:T(8,128)(2,1)})) %all-reduce.10.cloned.1.call-update) | async-done | bytes 491536 | tf_op jit(solution)/shard_map/psum | solution.py:135
  532.4 3.8 all-to-all-start
  538.2 4.4 all-to-all-done
  546.1 66.2 %all-gather.7.cloned.1.call-done = bf16[128,4,3072]{2,1,0:T(4,128)(2,1)} async-done(((bf16[1,4,3072]{2,1,0:T(4,128)(2,1)}), bf16[128,4,3072]{2,1,0:T(4,128)(2,1)}) %all-gather.7.cloned.1.call-update) | async-done | bytes 3145744 | tf_op jit(solution)/shard_map/all_gather | solution.py:194
  612.3 6.0 reshape.403
  618.3 3.2 fusion.56
  621.4 6.9 fusion.7
  629.7 7.2 all-gather.5.cloned.1.call-done
  636.9 4.1 bitcast_convert_fusion
  641.0 3.6 gather_fusion.2
  644.6 1.9 fusion.15
  646.5 153.9 %all-reduce.8.cloned.1.call-done = f32[512,3072]{1,0:T(8,128)} async-done(((f32[512,3072]{1,0:T(8,128)}), f32[512,3072]{1,0:T(8,128)}) %all-reduce.8.cloned.1.call-update) | async-done | bytes 6291472
  (189 shorter events, 123.2 us)
Async XLA Ops:
  7.2 5.3 copy-start
  7.2 523.0 %all-reduce.10.cloned.1.call-start = ((), (), s32[]{:S(2)}) async-start(), calls=%async_computation.4 | async-start | bytes 983040 | tf_op jit(solution)/shard_map/psum | solution.py:135
  22.5 110.6 %copy-start.10 = (f32[3072]{0:T(1024)S(1)}, f32[3072]{0:T(1024)}, u32[]{:S(2)}) copy-start(f32[3072]{0:T(1024)} %param.35) | copy-start | bytes 36868
  133.1 0.6 copy-start.5
  153.5 6.7 copy-start.12
  153.6 8.6 %copy-start.1 = (s32[32]{0:T(128)S(1)}, s32[32]{0:T(128)}, u32[]{:S(2)}) copy-start(s32[32]{0:T(128)} %param.30) | copy-start | bytes 388
  154.7 8.6 %copy-start.2 = (s32[32]{0:T(128)S(1)}, s32[32]{0:T(128)}, u32[]{:S(2)}) copy-start(s32[32]{0:T(128)} %param.33) | copy-start | bytes 388
  165.7 0.6 copy-start.8
  422.2 39.3 %copy-start.7 = (f32[4,16,6]{1,2,0:T(8,128)S(1)}, f32[4,16,6]{1,2,0:T(8,128)}, u32[]{:S(2)}) copy-start(f32[4,16,6]{1,2,0:T(8,128)} %pmax.7) | copy-start | bytes 4612
  422.2 108.0 %copy-start.9 = (bf16[4,16,1,128]{3,2,1,0:T(2,128)(2,1)S(1)}, bf16[4,16,1,128]{3,2,1,0:T(2,128)(2,1)}, u32[]{:S(2)}) copy-start(bf16[4,16,1,128]{3,2,1,0:T(2,128)(2,1)} %get-tuple-element.140) | copy-start | bytes 49156
  425.7 105.8 %copy-start.4 = (bf16[768,192]{0,1:T(8,128)(2,1)S(1)}, bf16[768,192]{0,1:T(8,128)(2,1)}, u32[]{:S(2)}) copy-start(bf16[768,192]{0,1:T(8,128)(2,1)} %param.40) | copy-start | bytes 884740
  427.9 114.9 %copy-start.6 = (bf16[4,3072]{1,0:T(4,128)(2,1)S(1)}, bf16[4,3072]{1,0:T(4,128)(2,1)}, u32[]{:S(2)}) copy-start(bf16[4,3072]{1,0:T(4,128)(2,1)} %copy-done.5) | copy-start | bytes 73732
  532.4 10.3 %all-to-all-start = ((bf16[16,4,192]{2,1,0:T(4,128)(2,1)}), bf16[16,4,192]{2,1,0:T(4,128)(2,1)S(1)}, u32[]{:S(2)}, u32[]{:S(2)}) async-start(bf16[16,4,192]{2,1,0:T(4,128)(2,1)} %all_to_all.10), calls=%async_computation | async-start | bytes 65536 | tf_op jit(solution)/shard_map/all_to_all | solution.py:159
  536.2 76.1 %all-gather.7.cloned.1.call-start = ((), (), s32[]{:S(2)}) async-start(), calls=%async_computation.2 | async-start | bytes 3170304 | tf_op jit(solution)/shard_map/all_gather | solution.py:194
  545.2 91.8 %all-gather.5.cloned.1.call-start = ((), (), s32[]{:S(2)}) async-start(), calls=%async_computation.1 | async-start | bytes 2359296 | tf_op jit(solution)/shard_map/all_gather | solution.py:202
  545.9 254.5 %all-reduce.8.cloned.1.call-start = ((), (), s32[]{:S(2)}) async-start(), calls=%async_computation.3 | async-start | bytes 12582912
  628.3 0.7 copy-start.11
  628.3 0.7 copy-start.3
Sparse Core Ops, SparseCore 0:
  431.5 98.6 all-reduce.9
  545.3 66.9 all-gather.6
  614.1 22.7 all-gather.4
  642.4 157.9 all-reduce.7
where the time goes:
time: 814 us; the launch traced here: 808 us
  waiting for transfers between devices  300 us (37%)
  blocking collectives  216 us (27%)
  other arithmetic  113 us (14%)
  local copies, waits for them, and re-layouts  112 us (14%)
  matrix products  35.8 us (4%)
  between operations  16.7 us (2%)
  loops' own time  9.92 us (1%)
    unnamed x5, waiting for transfers between devices  155 us
    unnamed x1, blocking collectives  110 us
    psum x1, waiting for transfers between devices, local(): lax.psum((local_out * factor[..., None]).astype(jnp.bfloat16), 'tok')  68 us
    all_gather x1, waiting for transfers between devices, local(): everything = lax.all_gather(second, ('req', 'tok'), axis=0, tiled=True)  66.2 us
    pmax x1, blocking collectives, local(): cache_max = lax.pmax(local_max, 'tok')  57.9 us
    reduce_sum x16, other arithmetic, advance(): readout = jnp.sum(current * step_read[:, None, None, :], axis=-1)  41 us
    select_n x16, other arithmetic, advance(): jnp.where((accept_count == step_index + 1)[:, None, None, None], current,...  31 us
    dynamic_slice x32, local copies, waits for them, and re-layouts, recurrence(): lax.scan(advance, (start_states, start_states), sequence)  30.9 us
  transfers between devices with their start and end apart: 5, of which 5 were waited for; matrix products, arithmetic and copies ran while one was open for 4% of the time, Pallas kernels for 0%

commit v1 on v0

--- a/solution.py
+++ b/solution.py
@@ -100,7 +100,22 @@
         tiled=True,
     ).astype(jnp.bfloat16)
     normed = rms_rows(embedded, mixer_gain)
-    gathered = lax.all_gather(normed, "tok", axis=0, tiled=True)
+    ways, here, step = (lax.axis_size("tok"), lax.axis_index("tok"), normed.shape[0])
+    shape = [n * ways if d == 0 else n for d, n in enumerate(normed.shape)]
+    gathered = lax.dynamic_update_slice_in_dim(
+        jnp.zeros(shape, normed.dtype), normed, here * step, axis=0
+    )
+    going_up = going_down = normed
+    for far in range(1, ways // 2 + 1):
+        going_up = lax.ppermute(going_up, "tok", [(d, (d + 1) % ways) for d in range(ways)])
+        gathered = lax.dynamic_update_slice_in_dim(
+            gathered, going_up, (here - far) % ways * step, axis=0
+        )
+        if 2 * far < ways:
+            going_down = lax.ppermute(going_down, "tok", [(d, (d - 1) % ways) for d in range(ways)])
+            gathered = lax.dynamic_update_slice_in_dim(
+                gathered, going_down, (here + far) % ways * step, axis=0
+            )
     queries = jnp.dot(gathered, query_weight, preferred_element_type=jnp.float32).astype(
         jnp.bfloat16
     )

time: 814 us -> 844 us (1.037)
  starting transfers between devices: 4.16 us -> 38.2 us
  blocking collectives: 216 us -> 194 us
  waiting for transfers between devices: 300 us -> 317 us
    ppermute x0 -> x15, starting transfers between devices: none -> 34.2 us  [the longest x7 33.1 us: local(): lax.ppermute(going_down, 'tok', [(d, (d - 1) % ways) for d in range(ways)])]
    all_gather x1 -> x0, blocking collectives: 19.8 us -> none  [local(): gathered = lax.all_gather(normed, 'tok', axis=0, tiled=True)]
    ppermute x0 -> x15, waiting for transfers between devices: none -> 11.1 us  [the longest x8 11 us: local(): lax.ppermute(going_up, 'tok', [(d, (d + 1) % ways) for d in range(ways)])]
  transfers between devices with their start and end apart: 5 -> 20, of which waited for: 5 -> 12; matrix products, arithmetic and copies ran while one was open for 4% -> 4% of each run, Pallas kernels for 0% -> 0%
where the time goes in v1:
time: 844 us; the launch traced here: 838 us
  waiting for transfers between devices  317 us (38%)
  blocking collectives  194 us (23%)
  other arithmetic  113 us (13%)
  local copies, waits for them, and re-layouts  111 us (13%)
  starting transfers between devices  38.2 us (5%)
  matrix products  35.9 us (4%)
  between operations  16.9 us (2%)
  loops' own time  10.1 us (1%)
    unnamed x5, waiting for transfers between devices  155 us
    unnamed x1, blocking collectives  110 us
    psum x1, waiting for transfers between devices, local(): lax.psum((local_out * factor[..., None]).astype(jnp.bfloat16), 'tok')  73.3 us
    all_gather x1, waiting for transfers between devices, local(): everything = lax.all_gather(second, ('req', 'tok'), axis=0, tiled=True)  66.3 us
    pmax x1, blocking collectives, local(): cache_max = lax.pmax(local_max, 'tok')  55.6 us
    reduce_sum x16, other arithmetic, advance(): readout = jnp.sum(current * step_read[:, None, None, :], axis=-1)  41 us
    ppermute x7, starting transfers between devices, local(): lax.ppermute(going_down, 'tok', [(d, (d - 1) % ways) for d in range(ways)])  33.1 us
    select_n x16, other arithmetic, advance(): jnp.where((accept_count == step_index + 1)[:, None, None, None], current,...  31.1 us
  transfers between devices with their start and end apart: 20, of which 12 were waited for; matrix products, arithmetic and copies ran while one was open for 4% of the time, Pallas kernels for 0%

profile of v1, /device:TPU:1, one launch (start us, length us, event | category | flops | bytes accessed | tf_op | source)
XLA Modules:
  0.0 837.5 jit_solution(12167083870177283595)
XLA Ops:
  7.2 2.0 copy.158
  12.3 3.9 gather_fusion.1
  16.2 6.2 convert_select_fusion
  22.4 109.7 %all-reduce.11 = bf16[512,3072]{1,0:T(8,128)(2,1)} all-reduce(f32[512,3072]{1,0:T(8,128)} %convert_select_fusion), channel_id=2, replica_groups=mesh['req'=8,'tok'=16] {'req','tok'}, use_global_device_ids=true, to_apply=%region_1.2.clone | all-reduce | flops 1572864 | bytes 9437184
  136.0 3.9 collective-permute-start.1
  149.4 4.8 collective-permute-start.3
  155.8 4.8 collective-permute-start.5
  161.8 4.8 collective-permute-start.7
  167.8 4.8 collective-permute-start.9
  173.8 5.1 collective-permute-start.11
  179.8 5.0 collective-permute-start.13
  185.8 5.9 collective-permute-done.14
  191.8 3.9 convolution_convert_fusion.1
  197.4 2.4 convolution_convert_fusion.2
  202.6 2.9 select_reduce_fusion
  205.5 55.6 %pmax.7 = f32[4,16,6]{1,2,0:T(8,128)} all-reduce(f32[4,16,6]{1,2,0:T(8,128)S(1)} %get-tuple-element.147), channel_id=1, replica_groups=mesh['req'=8,'tok'=16] {'tok'}, use_global_device_ids=true, to_apply=%region_4.6 | all-reduce | flops 384 | bytes 3072 | tf_op jit(solution)/shard_map/pmax | solution.py:146
  261.1 2.4 fusion.1
  263.5 3.2 fusion.54
  270.1 2.0 fusion.53
  281.2 165.4 %while.14 = (s32[]{:T(128)}, f32[4,1,128,256]{3,2,1,0:T(8,128)}, bf16[4,1,128,256]{3,2,1,0:T(8,128)(2,1)}, f32[16,4,1,128]{3,0,1,2:T(8,128)}, f32[16,4,1]{1,2,0:...) while((s32[]{:T(128)}, f32[4,1,128,256]{3,2,1,0:T(8,128)}, ...), condition=%wide.region_12.14_spmd, body=%wide.region_10.13_spmd.sunk | while | flops 785927 | bytes 2134257 | solution.py:39
  283.2 2.6 multiply_reduce_fusion.2
  288.3 1.9 broadcast_select_fusion.4
  293.6 2.6 multiply_reduce_fusion.2
  298.6 1.9 broadcast_select_fusion.4
  303.9 2.6 multiply_reduce_fusion.2
  308.9 1.9 broadcast_select_fusion.4
  314.2 2.6 multiply_reduce_fusion.2
  319.2 1.9 broadcast_select_fusion.4
  324.6 2.6 multiply_reduce_fusion.2
  329.6 1.9 broadcast_select_fusion.4
  334.9 2.6 multiply_reduce_fusion.2
  339.9 1.9 broadcast_select_fusion.4
  345.2 2.6 multiply_reduce_fusion.2
  350.3 1.9 broadcast_select_fusion.4
  355.6 2.6 multiply_reduce_fusion.2
  360.6 1.9 broadcast_select_fusion.4
  365.9 2.6 multiply_reduce_fusion.2
  370.9 1.9 broadcast_select_fusion.4
  376.3 2.6 multiply_reduce_fusion.2
  381.3 1.9 broadcast_select_fusion.4
  386.6 2.6 multiply_reduce_fusion.2
  391.7 1.9 broadcast_select_fusion.4
  396.9 2.6 multiply_reduce_fusion.2
  402.0 1.9 broadcast_select_fusion.4
  407.3 2.6 multiply_reduce_fusion.2
  417.6 2.6 multiply_reduce_fusion.2
  422.6 1.9 broadcast_select_fusion.4
  427.9 2.6 multiply_reduce_fusion.2
  438.2 2.6 multiply_reduce_fusion.2
  443.3 1.9 broadcast_select_fusion.4
  450.1 2.1 convolution_convert_fusion
  453.0 2.8 fusion.5
  455.8 29.0 %psum.15 = bf16[4,16,6]{1,2,0:T(8,128)(2,1)S(1)} all-reduce(bf16[4,16,6]{1,2,0:T(8,128)(2,1)S(1)} %get-tuple-element.132), channel_id=1, replica_groups=mesh['req'=8,'tok'=16] {'tok'}, use_global_device_ids=true, to_apply=%region_8.10 | all-reduce | flops 384 | bytes 1536 | tf_op jit(solution)/shard_map/psum | solution.py:149
  484.9 73.3 %all-reduce.10.cloned.1.call-done = (bf16[4,16,6,128]{3,1,2,0:T(8,128)(2,1)}, bf16[64,3072]{1,0:T(8,128)(2,1)}) async-done(((bf16[4,16,6,128]{3,1,2,0:T(8,128)(2,1)}, bf16[64,3072]{1,0:T(8,128)(2,1)}), (bf16[4,16,6,128]{3,1,2,0:T(8,128)(2,1)}, bf16[64,3072]{1,0:T(8,128)(2,1)})) %all-reduce.10.cloned.1.call-update) | async-done | bytes 491536 | tf_op jit(solution)/shard_map/psum | solution.py:150
  561.2 3.8 all-to-all-start
  567.0 4.5 all-to-all-done
  574.8 66.3 %all-gather.6.cloned.1.call-done = bf16[128,4,3072]{2,1,0:T(4,128)(2,1)} async-done(((bf16[1,4,3072]{2,1,0:T(4,128)(2,1)}), bf16[128,4,3072]{2,1,0:T(4,128)(2,1)}) %all-gather.6.cloned.1.call-update) | async-done | bytes 3145744 | tf_op jit(solution)/shard_map/all_gather | solution.py:209
  641.2 5.9 reshape.401
  647.1 3.1 fusion.56
  650.2 7.0 fusion.7
  658.5 7.3 all-gather.4.cloned.1.call-done
  665.8 4.0 bitcast_convert_fusion
  669.9 3.6 gather_fusion.2
  675.4 154.1 %all-reduce.8.cloned.1.call-done = f32[512,3072]{1,0:T(8,128)} async-done(((f32[512,3072]{1,0:T(8,128)}), f32[512,3072]{1,0:T(8,128)}) %all-reduce.8.cloned.1.call-update) | async-done | bytes 6291472
  (229 shorter events, 142.1 us)
Async XLA Ops:
  7.2 5.1 copy-start
  7.2 551.1 %all-reduce.10.cloned.1.call-start = ((), (), s32[]{:S(2)}) async-start(), calls=%async_computation.4 | async-start | bytes 983040 | tf_op jit(solution)/shard_map/psum | solution.py:150
  10.0 0.5 copy-start.9
  22.4 117.5 %copy-start.10 = (s32[32]{0:T(128)S(1)}, s32[32]{0:T(128)}, u32[]{:S(2)}) copy-start(s32[32]{0:T(128)} %param.32) | copy-start | bytes 388
  22.4 118.8 %copy-start.1 = (s32[32]{0:T(128)S(1)}, s32[32]{0:T(128)}, u32[]{:S(2)}) copy-start(s32[32]{0:T(128)} %param.30) | copy-start | bytes 388
  22.4 120.0 %copy-start.2 = (s32[32]{0:T(128)S(1)}, s32[32]{0:T(128)}, u32[]{:S(2)}) copy-start(s32[32]{0:T(128)} %param.33) | copy-start | bytes 388
  135.1 14.2 %collective-permute-start = (bf16[4,3072]{1,0:T(4,128)(2,1)}, bf16[4,3072]{1,0:T(4,128)(2,1)}, u32[]{:S(2)}, u32[]{:S(2)}) collective-permute-start(bf16[4,3072]{1,0:T(4,128)(2,1)} %get-tuple-element.135), channel_id=1, source_target_pairs={{0,1},{1,2},{2,3},{3,4},{4,5},{5,6},{6,7},{7,8},{8,9},{9,10},{10,1... | collective-permute-start | bytes 73736 | tf_op jit(solution)/shard_map/ppermute | solution.py:110
  136.0 13.4 %collective-permute-start.1 = (bf16[4,3072]{1,0:T(4,128)(2,1)}, bf16[4,3072]{1,0:T(4,128)(2,1)}, u32[]{:S(2)}, u32[]{:S(2)}) collective-permute-start(bf16[4,3072]{1,0:T(4,128)(2,1)} %get-tuple-element.135), channel_id=1, source_target_pairs={{0,15},{1,0},{2,1},{3,2},{4,3},{5,4},{6,5},{7,6},{8,7},{9,8},{10,9... | collective-permute-start | bytes 73736 | tf_op jit(solution)/shard_map/ppermute | solution.py:115
  149.3 6.4 collective-permute-start.2
  149.4 6.4 collective-permute-start.3
  155.7 6.1 collective-permute-start.4
  155.8 6.0 collective-permute-start.5
  161.8 6.0 collective-permute-start.6
  161.8 6.0 collective-permute-start.7
  167.8 6.0 collective-permute-start.8
  167.8 6.0 collective-permute-start.9
  173.8 6.0 collective-permute-start.10
  173.8 6.1 collective-permute-start.11
  179.8 6.0 collective-permute-start.12
  179.8 6.0 collective-permute-start.13
  185.8 6.0 collective-permute-start.14
  447.9 36.9 %copy-start.7 = (pred[16,16]{0,1:T(8,128)(4,1)S(1)}, pred[16,16]{0,1:T(8,128)(4,1)}, u32[]{:S(2)}) copy-start(pred[16,16]{0,1:T(8,128)(4,1)} %iota_compare_fusion.2) | copy-start | bytes 772
  448.0 37.0 %copy-start.5 = (f32[4,16,6]{1,2,0:T(8,128)S(1)}, f32[4,16,6]{1,2,0:T(8,128)}, u32[]{:S(2)}) copy-start(f32[4,16,6]{1,2,0:T(8,128)} %pmax.7) | copy-start | bytes 4612
  448.0 110.3 %copy-start.6 = (bf16[4,16,1,128]{3,2,1,0:T(2,128)(2,1)S(1)}, bf16[4,16,1,128]{3,2,1,0:T(2,128)(2,1)}, u32[]{:S(2)}) copy-start(bf16[4,16,1,128]{3,2,1,0:T(2,128)(2,1)} %get-tuple-element.142) | copy-start | bytes 49156
  452.2 119.4 %copy-start.4 = (bf16[4,3072]{1,0:T(4,128)(2,1)S(1)}, bf16[4,3072]{1,0:T(4,128)(2,1)}, u32[]{:S(2)}) copy-start(bf16[4,3072]{1,0:T(4,128)(2,1)} %get-tuple-element.137) | copy-start | bytes 73732
  561.2 10.3 %all-to-all-start = ((bf16[16,4,192]{2,1,0:T(4,128)(2,1)}), bf16[16,4,192]{2,1,0:T(4,128)(2,1)S(1)}, u32[]{:S(2)}, u32[]{:S(2)}) async-start(bf16[16,4,192]{2,1,0:T(4,128)(2,1)} %all_to_all.10), calls=%async_computation | async-start | bytes 65536 | tf_op jit(solution)/shard_map/all_to_all | solution.py:174
  565.1 76.1 %all-gather.6.cloned.1.call-start = ((), (), s32[]{:S(2)}) async-start(), calls=%async_computation.2 | async-start | bytes 3170304 | tf_op jit(solution)/shard_map/all_gather | solution.py:209
  574.0 91.8 %all-gather.4.cloned.1.call-start = ((), (), s32[]{:S(2)}) async-start(), calls=%async_computation.1 | async-start | bytes 2359296 | tf_op jit(solution)/shard_map/all_gather | solution.py:217
  574.8 254.7 %all-reduce.8.cloned.1.call-start = ((), (), s32[]{:S(2)}) async-start(), calls=%async_computation.3 | async-start | bytes 12582912
  657.2 0.6 copy-start.8
  657.2 0.7 copy-start.3
Sparse Core Ops, SparseCore 0:
  455.9 102.2 all-reduce.9
  574.2 66.9 all-gather.5
  643.0 22.7 all-gather.3
  671.2 158.1 all-reduce.7
